TPU v7x, 32 devices: a whole 2x2x4 slice. The times are simulated.
32 devices in a mesh: seq: 2 (over x), head: 4 (over z), pool: 4 (over y, core).
Axes of the slice: x: 2, y: 2, z: 4, core: 2. Of those that a mesh axis runs over, the one named last changes fastest.
Arguments:
- tokens: bfloat16 [32, 4096], P(('seq', 'head'), 'pool'), may hold values from -6 to 6
- routes: int32 [32, 8], P(('seq', 'head')), may hold values from 0 to 15, all different within a row; in each aligned block of 4 rows (0 to 3, 4 to 7, ...) at most 2 rows name the same one
- gate_fixed: int32 [32, 8], P(('seq', 'head')), may hold values from 1 to 65535
- gate_weight: bfloat16 [16, 4096, 3072], P('seq', 'pool', 'head'), may hold values from -0.09375 to 0.09375
- up_weight: bfloat16 [16, 4096, 3072], P('seq', 'pool', 'head'), may hold values from -0.09375 to 0.09375
- down_weight: bfloat16 [16, 3072, 4096], P('seq', 'head', 'pool'), may hold values from -0.109375 to 0.109375
- gate_scale: bfloat16 [16, 32, 24], P('seq', 'pool', 'head'), may hold values from 0.5 to 2
- up_scale: bfloat16 [16, 32, 24], P('seq', 'pool', 'head'), may hold values from 0.5 to 2
- down_scale: bfloat16 [16, 24, 32], P('seq', 'head', 'pool'), may hold values from 0.5 to 2
Outputs:
- combined: bfloat16 [32, 4096], P(('seq', 'head'), 'pool')
Inputs may be any that keep to these rules, and one draw needn't show every extreme that they name: `routes`: each row names 8 different experts. Within the rows of one device (aligned blocks of 4 rows) no expert is named by more than 2 rows, and in some blocks one expert is named by exactly 2 rows.
All inputs are finite; a program needn't handle non-finite values.
Results may differ from a plain program's by a relative error of at most 0.02.
Values may be sent and summed in bfloat16 or wider, within the bound.
No kernel may reach another device: no remote copies, remote signals or barrier semaphores. Data moves between devices by JAX's collectives and lax.ppermute only.
A program may use at most 128 MiB of HBM per device.

v0:
```python
import jax
import jax.numpy as jnp
from jax import lax
from jax.sharding import PartitionSpec as P

QB = 128
CAP = 2
largest_choice = lax.Precision.HIGHEST


def expand_scale(route_weight, scale):
    grown = jnp.repeat(jnp.repeat(scale, QB, axis=1), QB, axis=2)
    return route_weight * grown


def slot_positions(block_routes, expert_total):
    flattened = block_routes.reshape(-1)
    expert_ids = lax.broadcasted_iota(jnp.int32, (1, expert_total), 1)
    onehot = (flattened[:, None] == expert_ids).astype(jnp.int32)
    before = jnp.cumsum(onehot, axis=0) - onehot
    slot_index = jnp.sum(before * onehot, axis=1)
    return (flattened * CAP + slot_index).reshape(block_routes.shape)


def local_buffer(tokens, positions, slot_total):
    targets = lax.broadcasted_iota(jnp.int32, (slot_total, 1, 1), 0)
    selector = jnp.any(positions[None, :, :] == targets, axis=2).astype(jnp.bfloat16)
    return jnp.dot(selector, tokens, preferred_element_type=jnp.float32).astype(jnp.bfloat16)


def per_device(
    tokens,
    routes,
    gate_fixed,
    gate_weight,
    up_weight,
    down_weight,
    gate_scale,
    up_scale,
    down_scale,
):
    seq_count = lax.axis_size("seq")
    head_count = lax.axis_size("head")
    local_experts = gate_weight.shape[0]
    expert_total = local_experts * seq_count
    feature_width = tokens.shape[1]
    slot_total = expert_total * CAP
    block_total = seq_count * head_count
    gate_dense = expand_scale(gate_weight, gate_scale)
    up_dense = expand_scale(up_weight, up_scale)
    down_dense = expand_scale(down_weight, down_scale)
    positions = slot_positions(routes, expert_total)
    outgoing = local_buffer(tokens, positions, slot_total)
    outgoing = outgoing.reshape(seq_count, 1, local_experts, 1, CAP, feature_width)
    outgoing = jnp.broadcast_to(
        outgoing, (seq_count, head_count, local_experts, 1, CAP, feature_width)
    )
    outgoing = outgoing.reshape(block_total, local_experts, 1, CAP, feature_width)
    arrived = lax.all_to_all(outgoing, ("seq", "head"), split_axis=0, concat_axis=2, tiled=True)
    slot_rows = arrived.reshape(local_experts, seq_count, head_count, CAP, feature_width)
    gate_sum = jnp.einsum(
        "jshcd,jdf->jshcf", slot_rows, gate_dense, preferred_element_type=jnp.float32
    )
    up_sum = jnp.einsum("jshcd,jdf->jshcf", slot_rows, up_dense, preferred_element_type=jnp.float32)
    gate_sum, up_sum = (
        lax.psum(gate_sum.astype(jnp.bfloat16), "pool").astype(jnp.float32),
        lax.psum(up_sum.astype(jnp.bfloat16), "pool").astype(jnp.float32),
    )
    hidden = (jax.nn.silu(gate_sum) * up_sum).astype(jnp.bfloat16)
    partial_out = jnp.einsum(
        "jshcf,jfd->jshcd", hidden, down_dense, preferred_element_type=jnp.float32
    )
    sending = partial_out.astype(jnp.bfloat16).reshape(
        local_experts, block_total, CAP, feature_width
    )
    gathered_back = lax.all_to_all(
        sending, ("seq", "head"), split_axis=1, concat_axis=0, tiled=True
    )
    gathered_back = gathered_back.reshape(seq_count, head_count, local_experts, CAP, feature_width)
    results = jnp.sum(gathered_back.astype(jnp.float32), axis=1).astype(jnp.bfloat16)
    results = results.reshape(slot_total, feature_width)
    fixed = gate_fixed.astype(jnp.float32)
    weights = fixed / jnp.sum(fixed, axis=1, keepdims=True)
    slot_ids = lax.broadcasted_iota(jnp.int32, (1, 1, slot_total), 2)
    combine_weight = jnp.sum(
        jnp.where(positions[:, :, None] == slot_ids, weights[:, :, None], 0.0), axis=1
    )
    combined = jnp.dot(
        combine_weight,
        results.astype(jnp.float32),
        precision=largest_choice,
        preferred_element_type=jnp.float32,
    )
    return combined.astype(jnp.bfloat16)


def solution(mesh):
    return jax.shard_map(
        per_device,
        mesh=mesh,
        in_specs=(
            P(("seq", "head"), "pool"),
            P(("seq", "head"), None),
            P(("seq", "head"), None),
            P("seq", "pool", "head"),
            P("seq", "pool", "head"),
            P("seq", "head", "pool"),
            P("seq", "pool", "head"),
            P("seq", "pool", "head"),
            P("seq", "head", "pool"),
        ),
        out_specs=P(("seq", "head"), "pool"),
        check_vma=False,
    )
```

profile of v0, /device:TPU:0, one launch (start us, length us, event | category | flops | bytes accessed | tf_op | source)
XLA Modules:
  0.0 150.8 jit_solution(4185804847729853960)
XLA Ops:
  6.5 0.0 copy-start
  6.5 0.8 eq.20
  7.3 0.1 fusion.24
  7.4 0.1 reduce_window_sum.11
  7.4 0.2 select_reduce_fusion.1
  7.6 0.1 reduce_sum.42
  7.7 0.7 multiply_add_fusion
  8.4 0.1 fusion.25
  8.5 0.0 copy-done
  8.5 0.2 convolution_convert_fusion
  8.8 0.7 broadcast_in_dim.44
  9.5 7.3 %all-to-all-start = ((bf16[8,8,1,2,1024]{4,1,3,2,0:T(8,128)(2,1)}), bf16[8,8,1,2,1024]{4,1,3,2,0:T(8,128)(2,1)S(1)}, u32[]{:S(2)}, u32[]{:S(2)}) async-start(bf16[8,8,1,2,1024]{4,1,3,2,0:T(8,128)(2,1)} %bitcast), calls=%async_computation | async-start | bytes 524288 | tf_op jit(solution)/shard_map/all_to_all | solution.py:59
  16.8 0.0 copy-start.4
  16.8 0.0 all-reduce.3.cloned.1.call-start
  16.9 16.6 %copy.58 = bf16[8,1024,768]{1,2,0:T(8,128)(2,1)} copy(bf16[8,1024,768]{2,1,0:T(8,128)(2,1)} %param.12) | data formatting | bytes 25165824 | tf_op args[3]
  33.5 0.0 copy-done.4
  33.5 0.1 broadcast_in_dim.46
  33.7 0.1 copy.57
  33.7 0.0 copy-start.5
  33.8 16.6 %copy.62 = bf16[8,1024,768]{1,2,0:T(8,128)(2,1)} copy(bf16[8,1024,768]{2,1,0:T(8,128)(2,1)} %param.13) | data formatting | bytes 25165824 | tf_op args[4]
  50.4 0.0 copy-done.5
  50.4 0.1 broadcast_in_dim.48
  50.6 0.1 copy.61
  50.6 0.0 copy-start.3
  50.6 11.1 %bitcast_multiply_fusion.1 = bf16[8,1024,768]{1,2,0:T(8,128)(2,1)} fusion(bf16[8,1024,768]{1,2,0:T(8,128)(2,1)} %copy.58, bf16[8,1024,6]{1,2,0:T(8,128)(2,1)S(1)} %copy.57), kind=kLoop, calls=%fused_computation.7 | loop fusion | flops 6291456 | bytes 25264128 | tf_op jit(solution)/shard_map/mul | solution.py:13
  61.8 1.8 %copy-done.3 = bf16[8,1024,768]{1,2,0:T(8,128)(2,1)S(1)} copy-done((bf16[8,1024,768]{1,2,0:T(8,128)(2,1)S(1)}, bf16[8,1024,768]{1,2,0:T(8,128)(2,1)}, u32[]{:S(2)}) %copy-start.3) | copy-done | bytes 12582936
  63.5 5.2 %bitcast_multiply_fusion = bf16[8,1024,768]{1,2,0:T(8,128)(2,1)} fusion(bf16[8,1024,768]{1,2,0:T(8,128)(2,1)S(1)} %copy-done.3, bf16[8,1024,6]{1,2,0:T(8,128)(2,1)S(1)} %copy.61), kind=kLoop, calls=%fused_computation.6 | loop fusion | flops 6291456 | bytes 25264128 | tf_op jit(solution)/shard_map/mul | solution.py:13
  68.8 0.0 all-to-all-done
  68.8 8.9 %fusion.10 = bf16[8,2,4,2,768]{4,2,3,1,0:T(4,128)(2,1)} fusion(bf16[8,1024,768]{1,2,0:T(8,128)(2,1)} %bitcast_multiply_fusion.1, bf16[8,2,4,2,1024]{4,0,3,2,1:T(8,128)(2,1)S(1)} %bitcast.54), kind=kOutput, calls=%fused_computation.10 | convolution fusion | flops 201424896 | bytes 13041664 | tf_op jit(solution)/shard_map/jshcd,jdf->jshcf/dot_general | solution.py:61
  77.7 0.0 copy-done.2
  77.7 4.2 %fusion.13 = bf16[8,2,4,2,768]{4,2,3,1,0:T(4,128)(2,1)} fusion(bf16[8,1024,768]{1,2,0:T(8,128)(2,1)S(1)} %copy-done.2, bf16[8,2,4,2,1024]{4,0,3,2,1:T(8,128)(2,1)S(1)} %bitcast.55), kind=kOutput, calls=%fused_computation.11 | convolution fusion | flops 201424896 | bytes 13041664 | tf_op jit(solution)/shard_map/jshcd,jdf->jshcf/dot_general | solution.py:64
  81.9 0.0 all-reduce.3.cloned.1.call-update
  81.9 0.0 copy-done.6
  81.9 0.2 broadcast_in_dim.50
  82.1 8.9 %broadcast_in_dim.51 = bf16[8,768,8,128]{3,2,1,0:T(8,128)(2,1)} broadcast(bf16[8,768,8]{2,1,0:T(8,128)(2,1)S(1)} %bitcast.53), dimensions={0,1,2} | broadcast | bytes 12681216 | tf_op jit(solution)/shard_map/broadcast_in_dim | solution.py:12
  91.0 19.4 %reshape.62 = bf16[8,768,1024]{2,1,0:T(8,128)(2,1)} reshape(bf16[8,768,8,128]{3,2,1,0:T(8,128)(2,1)} %broadcast_in_dim.51) | data formatting | bytes 25165824 | tf_op jit(solution)/shard_map/reshape | solution.py:12
  110.4 6.0 %all-reduce.3.cloned.1.call-done = (bf16[8,2,4,2,768]{4,2,3,1,0:T(4,128)(2,1)}, bf16[8,2,4,2,768]{4,2,3,1,0:T(4,128)(2,1)}) async-done(((bf16[8,2,4,2,768]{4,2,3,1,0:T(4,128)(2,1)}, bf16[8,2,4,2,768]{4,2,3,1,0:T(4,128)(2,1)}), (bf16[8,2,4,2,768]{4,2,3,1,0:T(4,128)(2,1)}, bf16[8,2,4,2,768]{4,2,3,1,0:T(4,128)(2,1)})) %all-reduce.3.cloned.1.call-update) | async-done | bytes 393232 | tf_op jit(solution)/shard_map/psum | solution.py:67
  116.4 11.4 %fusion.7 = bf16[8,2,4,2,1024]{4,2,3,1,0:T(4,128)(2,1)S(1)} fusion(bf16[8,768,1024]{2,1,0:T(8,128)(2,1)} %param.14, bf16[8,768,1024]{2,1,0:T(8,128)(2,1)} %reshape.62, bf16[8,2,4,2,768]{4,2,3,1,0:T(4,128)(2,1)} %get-tuple-element.5, bf16[8,2,4,2,768]{4,2,3,1,0:T(4,128)(2,1)} %get-tuple-element.6), kind=kOutput, calls=%fused_computation.9 | convolution fusion | flops 208535552 | bytes 25821184 | tf_op jit(solution)/shard_map/jshcf,jfd->jshcd/dot_general | solution.py:70
  127.8 0.8 copy.66
  128.6 5.5 %all-to-all-start.1 = ((bf16[8,8,2,1024]{3,0,2,1:T(8,128)(2,1)}), bf16[8,8,2,1024]{3,0,2,1:T(8,128)(2,1)S(1)}, u32[]{:S(2)}, u32[]{:S(2)}) async-start(bf16[8,8,2,1024]{3,0,2,1:T(8,128)(2,1)} %bitcast.13), calls=%async_computation.1 | async-start | bytes 524288 | tf_op jit(solution)/shard_map/all_to_all | solution.py:76
  134.1 0.0 copy-done.7
  134.1 0.1 convert_reduce_fusion
  134.3 0.1 convert_divide_fusion
  134.3 0.1 select_reduce_fusion
  134.4 8.6 %all-to-all-done.1 = bf16[8,8,2,1024]{3,0,2,1:T(8,128)(2,1)S(1)} async-done(((bf16[8,8,2,1024]{3,0,2,1:T(8,128)(2,1)}), bf16[8,8,2,1024]{3,0,2,1:T(8,128)(2,1)S(1)}, u32[]{:S(2)}, u32[]{:S(2)}) %all-to-all-start.1) | async-done | bytes 262176 | tf_op jit(solution)/shard_map/all_to_all | solution.py:76
  143.1 0.1 copy.67
  143.2 0.8 convolution_convert_fusion.1
  143.9 0.0 copy-done.1
  (11 shorter events, 0.2 us)
Async XLA Ops:
  6.5 2.0 %copy-start = (bf16[4,1024]{1,0:T(4,128)(2,1)S(1)}, bf16[4,1024]{1,0:T(4,128)(2,1)}, u32[]{:S(2)}) copy-start(bf16[4,1024]{1,0:T(4,128)(2,1)} %param.9) | copy-start | bytes 24580
  9.5 59.3 %all-to-all-start = ((bf16[8,8,1,2,1024]{4,1,3,2,0:T(8,128)(2,1)}), bf16[8,8,1,2,1024]{4,1,3,2,0:T(8,128)(2,1)S(1)}, u32[]{:S(2)}, u32[]{:S(2)}) async-start(bf16[8,8,1,2,1024]{4,1,3,2,0:T(8,128)(2,1)} %bitcast), calls=%async_computation | async-start | bytes 524288 | tf_op jit(solution)/shard_map/all_to_all | solution.py:59
  16.8 16.7 %copy-start.4 = (bf16[8,8,6]{1,0,2:T(8,128)(2,1)S(1)}, bf16[8,8,6]{1,0,2:T(8,128)(2,1)}, u32[]{:S(2)}) copy-start(bf16[8,8,6]{1,0,2:T(8,128)(2,1)} %param.15) | copy-start | bytes 2308
  16.8 99.6 %all-reduce.3.cloned.1.call-start = ((), (), s32[]{:S(2)}) async-start(), calls=%async_computation.2 | async-start | bytes 786432 | tf_op jit(solution)/shard_map/psum | solution.py:67
  33.7 16.6 %copy-start.5 = (bf16[8,8,6]{1,0,2:T(8,128)(2,1)S(1)}, bf16[8,8,6]{1,0,2:T(8,128)(2,1)}, u32[]{:S(2)}) copy-start(bf16[8,8,6]{1,0,2:T(8,128)(2,1)} %param.16) | copy-start | bytes 2308
  50.6 12.9 %copy-start.3 = (bf16[8,1024,768]{1,2,0:T(8,128)(2,1)S(1)}, bf16[8,1024,768]{1,2,0:T(8,128)(2,1)}, u32[]{:S(2)}) copy-start(bf16[8,1024,768]{1,2,0:T(8,128)(2,1)} %copy.62) | copy-start | bytes 37748740
  68.8 8.9 %copy-start.2 = (bf16[8,1024,768]{1,2,0:T(8,128)(2,1)S(1)}, bf16[8,1024,768]{1,2,0:T(8,128)(2,1)}, u32[]{:S(2)}) copy-start(bf16[8,1024,768]{1,2,0:T(8,128)(2,1)} %bitcast_multiply_fusion) | copy-start | bytes 37748740
  68.8 13.1 %copy-start.6 = (bf16[8,6,8]{2,0,1:T(8,128)(2,1)S(1)}, bf16[8,6,8]{2,0,1:T(8,128)(2,1)}, u32[]{:S(2)}) copy-start(bf16[8,6,8]{2,0,1:T(8,128)(2,1)} %param.17) | copy-start | bytes 2308
  116.4 27.5 %copy-start.1 = (bf16[4,1024]{1,0:T(4,128)(2,1)S(1)}, bf16[4,1024]{1,0:T(4,128)(2,1)}, u32[]{:S(2)}) copy-start(bf16[4,1024]{1,0:T(4,128)(2,1)} %param.9) | copy-start | bytes 24580
  116.4 17.8 %copy-start.7 = (s32[4,8]{1,0:T(4,128)S(1)}, s32[4,8]{1,0:T(4,128)}, u32[]{:S(2)}) copy-start(s32[4,8]{1,0:T(4,128)} %param.11) | copy-start | bytes 388
  128.6 14.4 %all-to-all-start.1 = ((bf16[8,8,2,1024]{3,0,2,1:T(8,128)(2,1)}), bf16[8,8,2,1024]{3,0,2,1:T(8,128)(2,1)S(1)}, u32[]{:S(2)}, u32[]{:S(2)}) async-start(bf16[8,8,2,1024]{3,0,2,1:T(8,128)(2,1)} %bitcast.13), calls=%async_computation.1 | async-start | bytes 524288 | tf_op jit(solution)/shard_map/all_to_all | solution.py:76
Sparse Core Ops, SparseCore 0:
  82.0 34.2 all-reduce.2
where the time goes:
time: 152 us; the launch traced here: 151 us
  local copies, waits for them, and re-layouts  66.6 us (44%)
  matrix products  25.5 us (17%)
  other arithmetic  17.8 us (12%)
  waiting for transfers between devices  14.6 us (10%)
  between operations  13.5 us (9%)
  starting transfers between devices  12.8 us (8%)
    unnamed x19, local copies, waits for them, and re-layouts  35.1 us
    reshape x5, local copies, waits for them, and re-layouts, expand_scale(): grown = jnp.repeat(jnp.repeat(scale, QB, axis=1), QB, axis=2)  19.6 us
    mul x2, other arithmetic, expand_scale(): return route_weight * grown  16.4 us
    dot_general x1, matrix products, per_device(): jnp.einsum('jshcf,jfd->jshcd', hidden, down_dense, preferred_element_type...  11.4 us
    broadcast_in_dim x4, local copies, waits for them, and re-layouts, expand_scale(): grown = jnp.repeat(jnp.repeat(scale, QB, axis=1), QB, axis=2)  9.3 us
    dot_general x1, matrix products, per_device(): jnp.einsum('jshcd,jdf->jshcf', slot_rows, gate_dense, preferred_element_t...  8.89 us
    all_to_all x1, waiting for transfers between devices, per_device(): lax.all_to_all(sending, ('seq', 'head'), split_axis=1, concat_axis=0, til...  8.59 us
    all_to_all x1, starting transfers between devices, per_device(): lax.all_to_all(outgoing, ('seq', 'head'), split_axis=0, concat_axis=2, ti...  7.28 us
  transfers between devices with their start and end apart: 3, of which 2 were waited for; matrix products, arithmetic and copies ran while one was open for 52% of the time, Pallas kernels for 0%

commit v1 on v0

--- a/solution.py
+++ b/solution.py
@@ -73,8 +73,14 @@
     sending = partial_out.astype(jnp.bfloat16).reshape(
         local_experts, block_total, CAP, feature_width
     )
-    gathered_back = lax.all_to_all(
-        sending, ("seq", "head"), split_axis=1, concat_axis=0, tiled=True
+    gathered_back = jnp.concatenate(
+        lax.all_to_all(
+            jnp.stack(jnp.split(sending, lax.axis_size(("seq", "head")), axis=1)),
+            ("seq", "head"),
+            0,
+            0,
+        ),
+        axis=0,
     )
     gathered_back = gathered_back.reshape(seq_count, head_count, local_experts, CAP, feature_width)
     results = jnp.sum(gathered_back.astype(jnp.float32), axis=1).astype(jnp.bfloat16)

time: 152 us -> 157 us (1.033)
  local copies, waits for them, and re-layouts: 66.6 us -> 70.7 us
    unnamed x19 -> x26, local copies, waits for them, and re-layouts: 35.1 us -> 39.3 us
  transfers between devices with their start and end apart: 3 -> 3, of which waited for: 2 -> 2; matrix products, arithmetic and copies ran while one was open for 52% -> 51% of each run, Pallas kernels for 0% -> 0%
where the time goes in v1:
time: 157 us; the launch traced here: 155 us
  local copies, waits for them, and re-layouts  70.7 us (45%)
  matrix products  25.5 us (16%)
  other arithmetic  17.8 us (11%)
  waiting for transfers between devices  14.6 us (9%)
  between operations  13.6 us (9%)
  starting transfers between devices  12.8 us (8%)
    unnamed x26, local copies, waits for them, and re-layouts  39.3 us
    reshape x5, local copies, waits for them, and re-layouts, expand_scale(): grown = jnp.repeat(jnp.repeat(scale, QB, axis=1), QB, axis=2)  19.6 us
    mul x2, other arithmetic, expand_scale(): return route_weight * grown  16.4 us
    dot_general x1, matrix products, per_device(): jnp.einsum('jshcf,jfd->jshcd', hidden, down_dense, preferred_element_type...  11.4 us
    broadcast_in_dim x4, local copies, waits for them, and re-layouts, expand_scale(): grown = jnp.repeat(jnp.repeat(scale, QB, axis=1), QB, axis=2)  9.3 us
    dot_general x1, matrix products, per_device(): jnp.einsum('jshcd,jdf->jshcf', slot_rows, gate_dense, preferred_element_t...  8.89 us
    all_to_all x1, waiting for transfers between devices, per_device(): lax.all_to_all(jnp.stack(jnp.split(sending, lax.axis_size(('seq', 'head')...  8.59 us
    all_to_all x1, starting transfers between devices, per_device(): lax.all_to_all(outgoing, ('seq', 'head'), split_axis=0, concat_axis=2, ti...  7.28 us
  transfers between devices with their start and end apart: 3, of which 2 were waited for; matrix products, arithmetic and copies ran while one was open for 51% of the time, Pallas kernels for 0%

profile of v1, /device:TPU:0, one launch (start us, length us, event | category | flops | bytes accessed | tf_op | source)
XLA Modules:
  0.0 154.9 jit_solution(7704751971942306038)
XLA Ops:
  6.5 0.0 copy-start
  6.5 0.8 eq.20
  7.3 0.1 fusion.32
  7.4 0.1 reduce_window_sum.11
  7.4 0.2 select_reduce_fusion.1
  7.6 0.1 reduce_sum.42
  7.7 0.7 multiply_add_fusion
  8.4 0.1 fusion.33
  8.5 0.0 copy-done
  8.5 0.2 convolution_convert_fusion
  8.8 0.7 broadcast_in_dim.44
  9.5 7.3 %all-to-all-start = ((bf16[8,8,1,2,1024]{4,1,3,2,0:T(8,128)(2,1)}), bf16[8,8,1,2,1024]{4,1,3,2,0:T(8,128)(2,1)S(1)}, u32[]{:S(2)}, u32[]{:S(2)}) async-start(bf16[8,8,1,2,1024]{4,1,3,2,0:T(8,128)(2,1)} %bitcast), calls=%async_computation | async-start | bytes 524288 | tf_op jit(solution)/shard_map/all_to_all | solution.py:59
  16.8 0.0 all-reduce.3.cloned.1.call-start
  16.9 16.6 %copy.65 = bf16[8,1024,768]{1,2,0:T(8,128)(2,1)} copy(bf16[8,1024,768]{2,1,0:T(8,128)(2,1)} %param.12) | data formatting | bytes 25165824 | tf_op args[3]
  33.5 0.1 broadcast_in_dim.46
  33.7 0.1 copy.64
  33.7 0.0 copy-start.5
  33.8 16.6 %copy.69 = bf16[8,1024,768]{1,2,0:T(8,128)(2,1)} copy(bf16[8,1024,768]{2,1,0:T(8,128)(2,1)} %param.13) | data formatting | bytes 25165824 | tf_op args[4]
  50.4 0.1 broadcast_in_dim.48
  50.6 0.1 copy.68
  50.6 11.1 %bitcast_multiply_fusion.1 = bf16[8,1024,768]{1,2,0:T(8,128)(2,1)} fusion(bf16[8,1024,768]{1,2,0:T(8,128)(2,1)} %copy.65, bf16[8,1024,6]{1,2,0:T(8,128)(2,1)S(1)} %copy.64), kind=kLoop, calls=%fused_computation.7 | loop fusion | flops 6291456 | bytes 25264128 | tf_op jit(solution)/shard_map/mul | solution.py:13
  61.8 1.8 %copy-done.3 = bf16[8,1024,768]{1,2,0:T(8,128)(2,1)S(1)} copy-done((bf16[8,1024,768]{1,2,0:T(8,128)(2,1)S(1)}, bf16[8,1024,768]{1,2,0:T(8,128)(2,1)}, u32[]{:S(2)}) %copy-start.3) | copy-done | bytes 12582936
  63.5 5.2 %bitcast_multiply_fusion = bf16[8,1024,768]{1,2,0:T(8,128)(2,1)} fusion(bf16[8,1024,768]{1,2,0:T(8,128)(2,1)S(1)} %copy-done.3, bf16[8,1024,6]{1,2,0:T(8,128)(2,1)S(1)} %copy.68), kind=kLoop, calls=%fused_computation.6 | loop fusion | flops 6291456 | bytes 25264128 | tf_op jit(solution)/shard_map/mul | solution.py:13
  68.8 0.0 all-to-all-done
  68.8 8.9 %fusion.10 = bf16[8,2,4,2,768]{4,2,3,1,0:T(4,128)(2,1)} fusion(bf16[8,1024,768]{1,2,0:T(8,128)(2,1)} %bitcast_multiply_fusion.1, bf16[8,2,4,2,1024]{4,0,3,2,1:T(8,128)(2,1)S(1)} %bitcast.81), kind=kOutput, calls=%fused_computation.10 | convolution fusion | flops 201424896 | bytes 13041664 | tf_op jit(solution)/shard_map/jshcd,jdf->jshcf/dot_general | solution.py:61
  77.7 4.2 %fusion.13 = bf16[8,2,4,2,768]{4,2,3,1,0:T(4,128)(2,1)} fusion(bf16[8,1024,768]{1,2,0:T(8,128)(2,1)S(1)} %copy-done.2, bf16[8,2,4,2,1024]{4,0,3,2,1:T(8,128)(2,1)S(1)} %bitcast.82), kind=kOutput, calls=%fused_computation.11 | convolution fusion | flops 201424896 | bytes 13041664 | tf_op jit(solution)/shard_map/jshcd,jdf->jshcf/dot_general | solution.py:64
  81.9 0.0 all-reduce.3.cloned.1.call-update
  81.9 0.2 broadcast_in_dim.50
  82.1 8.9 %broadcast_in_dim.51 = bf16[8,768,8,128]{3,2,1,0:T(8,128)(2,1)} broadcast(bf16[8,768,8]{2,1,0:T(8,128)(2,1)S(1)} %bitcast.80), dimensions={0,1,2} | broadcast | bytes 12681216 | tf_op jit(solution)/shard_map/broadcast_in_dim | solution.py:12
  91.0 19.4 %reshape.58 = bf16[8,768,1024]{2,1,0:T(8,128)(2,1)} reshape(bf16[8,768,8,128]{3,2,1,0:T(8,128)(2,1)} %broadcast_in_dim.51) | data formatting | bytes 25165824 | tf_op jit(solution)/shard_map/reshape | solution.py:12
  110.4 6.0 %all-reduce.3.cloned.1.call-done = (bf16[8,2,4,2,768]{4,2,3,1,0:T(4,128)(2,1)}, bf16[8,2,4,2,768]{4,2,3,1,0:T(4,128)(2,1)}) async-done(((bf16[8,2,4,2,768]{4,2,3,1,0:T(4,128)(2,1)}, bf16[8,2,4,2,768]{4,2,3,1,0:T(4,128)(2,1)}), (bf16[8,2,4,2,768]{4,2,3,1,0:T(4,128)(2,1)}, bf16[8,2,4,2,768]{4,2,3,1,0:T(4,128)(2,1)})) %all-reduce.3.cloned.1.call-update) | async-done | bytes 393232 | tf_op jit(solution)/shard_map/psum | solution.py:67
  116.4 11.4 %fusion.7 = bf16[8,2,4,2,1024]{4,2,3,1,0:T(4,128)(2,1)S(1)} fusion(bf16[8,768,1024]{2,1,0:T(8,128)(2,1)} %param.14, bf16[8,768,1024]{2,1,0:T(8,128)(2,1)} %reshape.58, bf16[8,2,4,2,768]{4,2,3,1,0:T(4,128)(2,1)} %get-tuple-element.5, bf16[8,2,4,2,768]{4,2,3,1,0:T(4,128)(2,1)} %get-tuple-element.6), kind=kOutput, calls=%fused_computation.9 | convolution fusion | flops 208535552 | bytes 25821184 | tf_op jit(solution)/shard_map/jshcf,jfd->jshcd/dot_general | solution.py:70
  127.8 0.2 copy.73
  127.9 0.6 fusion.31
  128.5 0.6 fusion.30
  129.1 0.6 fusion.29
  129.7 0.6 fusion.28
  130.4 0.6 fusion.27
  131.0 0.6 fusion.26
  131.6 0.6 fusion.25
  132.2 0.6 fusion.24
  132.8 5.5 %all-to-all-start.1 = ((bf16[8,8,1,2,1024]{4,1,3,2,0:T(8,128)(2,1)}), bf16[8,8,1,2,1024]{4,1,3,2,0:T(8,128)(2,1)S(1)}, u32[]{:S(2)}, u32[]{:S(2)}) async-start(bf16[8,8,1,2,1024]{4,1,3,2,0:T(8,128)(2,1)} %fusion.24), calls=%async_computation.1 | async-start | bytes 524288 | tf_op jit(solution)/shard_map/all_to_all | solution.py:77
  138.3 0.1 convert_reduce_fusion
  138.4 0.1 convert_divide_fusion
  138.5 0.1 select_reduce_fusion
  138.6 8.6 %all-to-all-done.1 = bf16[8,8,1,2,1024]{4,1,3,2,0:T(8,128)(2,1)S(1)} async-done(((bf16[8,8,1,2,1024]{4,1,3,2,0:T(8,128)(2,1)}), bf16[8,8,1,2,1024]{4,1,3,2,0:T(8,128)(2,1)S(1)}, u32[]{:S(2)}, u32[]{:S(2)}) %all-to-all-start.1) | async-done | bytes 262176 | tf_op jit(solution)/shard_map/all_to_all | solution.py:77
  147.2 0.1 copy.74
  147.3 0.8 convolution_convert_fusion.1
  (19 shorter events, 0.2 us)
Async XLA Ops:
  6.5 2.0 %copy-start = (bf16[4,1024]{1,0:T(4,128)(2,1)S(1)}, bf16[4,1024]{1,0:T(4,128)(2,1)}, u32[]{:S(2)}) copy-start(bf16[4,1024]{1,0:T(4,128)(2,1)} %param.9) | copy-start | bytes 24580
  9.5 59.3 %all-to-all-start = ((bf16[8,8,1,2,1024]{4,1,3,2,0:T(8,128)(2,1)}), bf16[8,8,1,2,1024]{4,1,3,2,0:T(8,128)(2,1)S(1)}, u32[]{:S(2)}, u32[]{:S(2)}) async-start(bf16[8,8,1,2,1024]{4,1,3,2,0:T(8,128)(2,1)} %bitcast), calls=%async_computation | async-start | bytes 524288 | tf_op jit(solution)/shard_map/all_to_all | solution.py:59
  16.8 16.7 %copy-start.4 = (bf16[8,8,6]{1,0,2:T(8,128)(2,1)S(1)}, bf16[8,8,6]{1,0,2:T(8,128)(2,1)}, u32[]{:S(2)}) copy-start(bf16[8,8,6]{1,0,2:T(8,128)(2,1)} %param.15) | copy-start | bytes 2308
  16.8 99.6 %all-reduce.3.cloned.1.call-start = ((), (), s32[]{:S(2)}) async-start(), calls=%async_computation.2 | async-start | bytes 786432 | tf_op jit(solution)/shard_map/psum | solution.py:67
  33.7 16.6 %copy-start.5 = (bf16[8,8,6]{1,0,2:T(8,128)(2,1)S(1)}, bf16[8,8,6]{1,0,2:T(8,128)(2,1)}, u32[]{:S(2)}) copy-start(bf16[8,8,6]{1,0,2:T(8,128)(2,1)} %param.16) | copy-start | bytes 2308
  50.6 12.9 %copy-start.3 = (bf16[8,1024,768]{1,2,0:T(8,128)(2,1)S(1)}, bf16[8,1024,768]{1,2,0:T(8,128)(2,1)}, u32[]{:S(2)}) copy-start(bf16[8,1024,768]{1,2,0:T(8,128)(2,1)} %copy.69) | copy-start | bytes 37748740
  68.8 8.9 %copy-start.2 = (bf16[8,1024,768]{1,2,0:T(8,128)(2,1)S(1)}, bf16[8,1024,768]{1,2,0:T(8,128)(2,1)}, u32[]{:S(2)}) copy-start(bf16[8,1024,768]{1,2,0:T(8,128)(2,1)} %bitcast_multiply_fusion) | copy-start | bytes 37748740
  68.8 13.1 %copy-start.6 = (bf16[8,6,8]{2,0,1:T(8,128)(2,1)S(1)}, bf16[8,6,8]{2,0,1:T(8,128)(2,1)}, u32[]{:S(2)}) copy-start(bf16[8,6,8]{2,0,1:T(8,128)(2,1)} %param.17) | copy-start | bytes 2308
  116.4 31.7 %copy-start.1 = (bf16[4,1024]{1,0:T(4,128)(2,1)S(1)}, bf16[4,1024]{1,0:T(4,128)(2,1)}, u32[]{:S(2)}) copy-start(bf16[4,1024]{1,0:T(4,128)(2,1)} %param.9) | copy-start | bytes 24580
  116.4 21.9 %copy-start.7 = (s32[4,8]{1,0:T(4,128)S(1)}, s32[4,8]{1,0:T(4,128)}, u32[]{:S(2)}) copy-start(s32[4,8]{1,0:T(4,128)} %param.11) | copy-start | bytes 388
  132.8 14.4 %all-to-all-start.1 = ((bf16[8,8,1,2,1024]{4,1,3,2,0:T(8,128)(2,1)}), bf16[8,8,1,2,1024]{4,1,3,2,0:T(8,128)(2,1)S(1)}, u32[]{:S(2)}, u32[]{:S(2)}) async-start(bf16[8,8,1,2,1024]{4,1,3,2,0:T(8,128)(2,1)} %fusion.24), calls=%async_computation.1 | async-start | bytes 524288 | tf_op jit(solution)/shard_map/all_to_all | solution.py:77
Sparse Core Ops, SparseCore 0:
  82.0 34.2 all-reduce.2
